TPU v7x, 32 devices: a whole 2x2x4 slice. The times are simulated.
32 devices in a mesh: groups: 2 (over x), expert: 16 (over z, y, core).
Axes of the slice: x: 2, y: 2, z: 4, core: 2. Of those that a mesh axis runs over, the one named last changes fastest.
Arguments:
- tokens: bfloat16 [2, 2048, 2048], P(None, ('groups', 'expert')), parts along dimension 1, may hold values from -6 to 6
- w_gate: bfloat16 [16, 2048, 768], P('expert'), may hold values from -0.125 to 0.125
- w_up: bfloat16 [16, 2048, 768], P('expert'), may hold values from -0.125 to 0.125
- w_down: bfloat16 [16, 768, 2048], P('expert'), may hold values from -0.21875 to 0.21875
- hot_gate: bfloat16 [2, 2048, 768], P(None, None, 'expert'), may hold values from -0.125 to 0.125
- hot_up: bfloat16 [2, 2048, 768], P(None, None, 'expert'), may hold values from -0.125 to 0.125
- hot_down: bfloat16 [2, 2048, 768], P(None, None, 'expert'), may hold values from -0.21875 to 0.21875
- cold_routes: int32 [2, 2048, 7], P(None, ('groups', 'expert')), parts along dimension 1, may hold values from 0 to 15, all different within a row; in each aligned block of 64 rows (0 to 63, 64 to 127, ..., all dimensions but the last counted through in order) at most 43 rows name the same one
- hot_pick: int32 [2, 2048], P(None, ('groups', 'expert')), parts along dimension 1, may hold values from 0 to 1, as said below
- gates: float32 [2, 2048, 8], P(None, ('groups', 'expert')), parts along dimension 1, may hold values from 0.1 to 1
Outputs:
- mixed: bfloat16 [2, 2048, 2048], P(None, ('groups', 'expert')), parts along dimension 1
There are 2 independent parts, one for each index of `groups`. A program takes and returns all parts, laid end to end along the dimension named above; an argument that names none is the same for every part. Nothing has to cross between parts.
Inputs may be any that keep to these rules, and one draw needn't show every extreme that they name: `hot_pick`: in each aligned block of 64 tokens of one micro-batch, each hot expert is picked by exactly 32 tokens. `cold_routes`: A token names 8 - 1 different cold experts; in each aligned block of 64 tokens of one micro-batch no cold expert is named more than 43 times.
All inputs are finite; a program needn't handle non-finite values.
Results may differ from a plain program's by a relative error of at most 0.0058.
Values may be sent and summed in bfloat16 or wider, within the bound.
A program may use at most 128 MiB of HBM per device.

v0:
```python
import jax
import jax.numpy as jnp
from jax import lax
from jax.sharding import PartitionSpec as P

TOP = 8
HOT = 2


def expert_rows(rows_in, weights):
    leading = rows_in.shape[:-1]
    flat_rows = rows_in.reshape(-1, rows_in.shape[-1])
    gate = jnp.dot(flat_rows, weights[0], preferred_element_type=jnp.float32)
    upward = jnp.dot(flat_rows, weights[1], preferred_element_type=jnp.float32)
    hidden = (jax.nn.silu(gate) * upward).astype(jnp.bfloat16)
    result = jnp.dot(hidden, weights[2], preferred_element_type=jnp.float32).astype(jnp.bfloat16)
    return result.reshape(leading + (result.shape[-1],))


def slot_table(routes_block, axis_width, capacity):
    expert = routes_block.reshape(-1)
    total_count = expert.shape[0]
    onehot = (expert[:, None] == jnp.arange(axis_width, dtype=jnp.int32)[None, :]).astype(jnp.int32)
    before = jnp.cumsum(onehot, axis=0) - onehot
    slot_rank = jnp.sum(before * onehot, axis=1)
    slot_place = expert * capacity + slot_rank
    target = jnp.arange(axis_width * capacity, dtype=jnp.int32)
    matched = slot_place[None, :] == target[:, None]
    filled = jnp.any(matched, axis=1)
    source = jnp.sum(
        jnp.where(matched, jnp.arange(total_count, dtype=jnp.int32)[None, :], 0), axis=1
    )
    return (slot_place, source, filled)


def shards(tokens, w_gate, w_up, w_down, hot_gate, hot_up, hot_down, cold_routes, hot_pick, gates):
    axis_width = lax.axis_size("expert")
    micro_count, local_tokens, model_width = tokens.shape
    picks = TOP - 1
    capacity = local_tokens * picks * 3 // (2 * axis_width) + 1
    own_weights = (w_gate[0], w_up[0], w_down[0])
    outbound = []
    tables = []
    for micro in range(micro_count):
        slot_place, source, filled = slot_table(cold_routes[micro], axis_width, capacity)
        rows_out = tokens[micro][source // picks]
        rows_out = jnp.where(filled[:, None], rows_out, jnp.zeros_like(rows_out))
        outbound.append(rows_out.reshape(axis_width, capacity, model_width))
        tables.append(slot_place)
    joined = jnp.concatenate(outbound, axis=1)
    back_all = lax.all_to_all(
        expert_rows(
            lax.all_to_all(joined, "expert", split_axis=0, concat_axis=0, tiled=True), own_weights
        ),
        "expert",
        split_axis=0,
        concat_axis=0,
        tiled=True,
    )
    returned = [
        back_all[:, micro * capacity : (micro + 1) * capacity] for micro in range(micro_count)
    ]
    cold_parts = []
    for micro in range(micro_count):
        picked = returned[micro].reshape(axis_width * capacity, model_width)[tables[micro]]
        picked = picked.reshape(local_tokens, picks, model_width).astype(jnp.float32)
        cold_parts.append(jnp.sum(picked * gates[micro, :, 1:, None], axis=1))
    cold_total = jnp.stack(cold_parts)
    all_rows = micro_count * local_tokens
    flat = tokens.reshape(all_rows, model_width)
    order = jnp.argsort(hot_pick.reshape(all_rows), stable=True)
    share = all_rows // HOT
    grouped = flat[order].reshape(HOT, share, model_width)
    gate = jnp.einsum(
        "hsd,hdf->hsf",
        grouped,
        lax.all_gather(hot_gate, "expert", axis=2, tiled=True),
        preferred_element_type=jnp.float32,
    )
    upward = jnp.einsum(
        "hsd,hdf->hsf",
        grouped,
        lax.all_gather(hot_up, "expert", axis=2, tiled=True),
        preferred_element_type=jnp.float32,
    )
    hidden = (jax.nn.silu(gate) * upward).astype(jnp.bfloat16)
    hot_sum = jnp.einsum(
        "hsf,hdf->hsd",
        hidden,
        lax.all_gather(hot_down, "expert", axis=2, tiled=True),
        preferred_element_type=jnp.float32,
    )
    sorted_out = hot_sum.astype(jnp.bfloat16).reshape(all_rows, model_width)
    inverse = jnp.argsort(order)
    hot_out = sorted_out[inverse].astype(jnp.float32) * gates[:, :, 0].reshape(all_rows)[:, None]
    total = hot_out.reshape(micro_count, local_tokens, model_width) + cold_total
    return total.astype(jnp.bfloat16)


def solution(mesh):
    in_specs = (
        P(None, ("groups", "expert"), None),
        P("expert", None, None),
        P("expert", None, None),
        P("expert", None, None),
        P(None, None, "expert"),
        P(None, None, "expert"),
        P(None, None, "expert"),
        P(None, ("groups", "expert"), None),
        P(None, ("groups", "expert")),
        P(None, ("groups", "expert"), None),
    )
    out_specs = P(None, ("groups", "expert"), None)
    return jax.shard_map(shards, mesh=mesh, in_specs=in_specs, out_specs=out_specs, check_vma=False)
```

profile of v0, /device:TPU:13, one launch (start us, length us, event | category | flops | bytes accessed | tf_op | source)
XLA Modules:
  0.0 446.5 jit_solution(14287439265493396799)
XLA Ops:
  9.1 1.2 reduce-window.14
  13.2 1.8 slice_bitcast_fusion.1
  15.0 8.0 %gather_fusion.2 = bf16[688,2048]{1,0:T(8,128)(2,1)} fusion(bf16[64,2048]{1,0:T(8,128)(2,1)} %get-tuple-element.11, s32[1024]{0:T(1024)S(1)} %pad_clamp_fusion.3), kind=kCustom, calls=%fused_computation.2 | custom fusion | bytes 5638848 | tf_op jit(solution)/shard_map/gather | solution.py:46
  23.0 3.5 gather.25
  26.5 4.1 gather_fusion.3
  30.6 3.5 gather.27
  34.5 3.1 broadcast_select_fusion
  37.7 4.1 pad_maximum_fusion
  41.8 6.5 %all-to-all-start = ((bf16[16,86,2048]{2,1,0:T(8,128)(2,1)}), bf16[16,86,2048]{2,1,0:T(8,128)(2,1)}, u32[]{:S(2)}, u32[]{:S(2)}) async-start(bf16[16,86,2048]{2,1,0:T(8,128)(2,1)} %pad_maximum_fusion), calls=%async_computation | async-start | bytes 11534336 | tf_op jit(solution)/shard_map/all_to_all | solution.py:53
  49.1 180.3 %all-to-all-done = bf16[16,86,2048]{2,1,0:T(8,128)(2,1)} async-done(((bf16[16,86,2048]{2,1,0:T(8,128)(2,1)}), bf16[16,86,2048]{2,1,0:T(8,128)(2,1)}, u32[]{:S(2)}, u32[]{:S(2)}) %all-to-all-start) | async-done | bytes 5636128 | tf_op jit(solution)/shard_map/all_to_all | solution.py:53
  229.4 6.2 %reshape.256 = bf16[1376,2048]{1,0:T(8,128)(2,1)} reshape(bf16[16,86,2048]{2,1,0:T(8,128)(2,1)} %all-to-all-done) | data formatting | bytes 11272192 | tf_op jit(solution)/shard_map/reshape | solution.py:12
  235.6 7.7 %fusion.2 = f32[1376,768]{1,0:T(8,128)S(1)} fusion(bf16[1376,2048]{1,0:T(8,128)(2,1)} %reshape.256, bf16[1,2048,768]{2,1,0:T(8,128)(2,1)} %param.11), kind=kOutput, calls=%fused_computation.13 | convolution fusion | flops 4328521728 | bytes 13008896 | tf_op jit(solution)/shard_map/dot_general | solution.py:13
  243.3 5.0 %multiply_convert_fusion = bf16[1376,768]{1,0:T(8,128)(2,1)S(1)} fusion(f32[1376,768]{1,0:T(8,128)S(1)} %fusion.2, bf16[1376,2048]{1,0:T(8,128)(2,1)S(1)} %copy-done.4, bf16[1,2048,768]{2,1,0:T(8,128)(2,1)S(1)} %copy-done.7), kind=kOutput, calls=%fused_computation.8 | convolution fusion | flops 4334862336 | bytes 15122432 | tf_op jit(solution)/shard_map/dot_general | solution.py:14
  248.4 6.4 %convolution_convert_fusion = bf16[1376,2048]{1,0:T(8,128)(2,1)} fusion(bf16[1376,768]{1,0:T(8,128)(2,1)S(1)} %multiply_convert_fusion, bf16[1,768,2048]{2,1,0:T(8,128)(2,1)S(1)} %copy-done), kind=kOutput, calls=%fused_computation.6 | convolution fusion | flops 4331339776 | bytes 10895360 | tf_op jit(solution)/shard_map/dot_general | solution.py:16
  254.8 6.2 %reshape.257 = bf16[16,86,2048]{2,1,0:T(8,128)(2,1)} reshape(bf16[1376,2048]{1,0:T(8,128)(2,1)} %convolution_convert_fusion) | data formatting | bytes 11272192 | tf_op jit(solution)/shard_map/reshape | solution.py:17
  261.1 5.5 %all-to-all-start.1 = ((bf16[16,86,2048]{2,1,0:T(8,128)(2,1)}), bf16[16,86,2048]{2,1,0:T(8,128)(2,1)}, u32[]{:S(2)}, u32[]{:S(2)}) async-start(bf16[16,86,2048]{2,1,0:T(8,128)(2,1)} %reshape.257), calls=%async_computation.1 | async-start | bytes 11534336 | tf_op jit(solution)/shard_map/all_to_all | solution.py:51
  267.3 2.5 sort.34
  269.9 2.5 sort.35
  273.5 4.8 %fusion.25 = f32[2,64,768]{2,1,0:T(8,128)S(1)} fusion(bf16[2,64,2048]{2,1,0:T(8,128)(2,1)S(1)} %bitcast.63, bf16[2,2048,768]{1,2,0:T(8,128)(2,1)} %all-gather.4.cloned.1.call-done), kind=kOutput, calls=%fused_computation.90 | convolution fusion | flops 402653184 | bytes 7208960 | tf_op jit(solution)/shard_map/hsd,hdf->hsf/dot_general | solution.py:74
  278.3 46.1 %all-gather.8.cloned.1.call-done = bf16[2,2048,768]{1,2,0:T(8,128)(2,1)} async-done(((bf16[2,2048,48]{1,2,0:T(8,128)(2,1)}), bf16[2,2048,768]{1,2,0:T(8,128)(2,1)}) %all-gather.8.cloned.1.call-update) | async-done | bytes 6291472 | tf_op jit(solution)/shard_map/all_gather | solution.py:90
  324.4 7.7 %convolution_convert_fusion.1 = bf16[2,64,2048]{2,1,0:T(8,128)(2,1)S(1)} fusion(bf16[2,2048,768]{1,2,0:T(8,128)(2,1)} %all-gather.8.cloned.1.call-done, bf16[2,64,2048]{2,1,0:T(8,128)(2,1)S(1)} %bitcast.64, bf16[2,2048,768]{1,2,0:T(8,128)(2,1)} %all-gather.6.cloned.1.call-done, f32[2,64,768]{2,1,0:T(8,128)S(1)} %fusion.25), kind=kOutput, calls=%fused_computation.17 | convolution fusion | flops 806158336 | bytes 14024704 | tf_op jit(solution)/shard_map/hsf,hdf->hsd/dot_general | solution.py:87
  332.2 1.7 gather_fusion.1
  333.9 73.7 %all-to-all-done.1 = bf16[16,86,2048]{2,1,0:T(8,128)(2,1)} async-done(((bf16[16,86,2048]{2,1,0:T(8,128)(2,1)}), bf16[16,86,2048]{2,1,0:T(8,128)(2,1)}, u32[]{:S(2)}, u32[]{:S(2)}) %all-to-all-start.1) | async-done | bytes 5636128 | tf_op jit(solution)/shard_map/all_to_all | solution.py:51
  407.6 7.3 %fusion.23 = (bf16[16,43,2048]{2,1,0:T(8,128)(2,1)}, bf16[16,43,2048]{2,1,0:T(8,128)(2,1)}) fusion(bf16[16,86,2048]{2,1,0:T(8,128)(2,1)} %all-to-all-done.1), kind=kLoop, calls=%fused_computation.88 | loop fusion | bytes 11272192 | tf_op jit(solution)/shard_map/slice | solution.py:61
  414.9 2.3 reshape.258
  417.2 3.3 gather_fusion.4
  420.5 3.8 reshape.263
  424.2 2.3 reshape.259
  426.6 3.2 gather_fusion.5
  429.8 3.8 reshape.264
  433.5 3.9 multiply_reduce_fusion.1
  437.5 1.5 multiply_reduce_fusion
  (85 shorter events, 9.4 us)
Async XLA Ops:
  6.5 241.9 %copy-start = (bf16[1,768,2048]{2,1,0:T(8,128)(2,1)S(1)}, bf16[1,768,2048]{2,1,0:T(8,128)(2,1)}, u32[]{:S(2)}) copy-start(bf16[1,768,2048]{2,1,0:T(8,128)(2,1)} %param.13) | copy-start | bytes 9437188
  6.5 266.9 %all-gather.4.cloned.1.call-start = ((), (), s32[]{:S(2)}) async-start(), calls=%async_computation.2 | async-start | bytes 6684672 | tf_op jit(solution)/shard_map/all_gather | solution.py:77
  7.3 271.0 %all-gather.6.cloned.1.call-start = ((), (), s32[]{:S(2)}) async-start(), calls=%async_computation.3 | async-start | bytes 6684672 | tf_op jit(solution)/shard_map/all_gather | solution.py:83
  41.8 187.6 %all-to-all-start = ((bf16[16,86,2048]{2,1,0:T(8,128)(2,1)}), bf16[16,86,2048]{2,1,0:T(8,128)(2,1)}, u32[]{:S(2)}, u32[]{:S(2)}) async-start(bf16[16,86,2048]{2,1,0:T(8,128)(2,1)} %pad_maximum_fusion), calls=%async_computation | async-start | bytes 11534336 | tf_op jit(solution)/shard_map/all_to_all | solution.py:53
  48.3 276.1 %all-gather.8.cloned.1.call-start = ((), (), s32[]{:S(2)}) async-start(), calls=%async_computation.4 | async-start | bytes 6684672 | tf_op jit(solution)/shard_map/all_gather | solution.py:90
  235.6 7.7 %copy-start.4 = (bf16[1376,2048]{1,0:T(8,128)(2,1)S(1)}, bf16[1376,2048]{1,0:T(8,128)(2,1)}, u32[]{:S(2)}) copy-start(bf16[1376,2048]{1,0:T(8,128)(2,1)} %reshape.256) | copy-start | bytes 16908292
  235.6 7.7 %copy-start.7 = (bf16[1,2048,768]{2,1,0:T(8,128)(2,1)S(1)}, bf16[1,2048,768]{2,1,0:T(8,128)(2,1)}, u32[]{:S(2)}) copy-start(bf16[1,2048,768]{2,1,0:T(8,128)(2,1)} %param.12) | copy-start | bytes 9437188
  261.0 5.7 %copy-start.6 = (f32[2,64,8]{1,2,0:T(8,128)S(1)}, f32[2,64,8]{1,2,0:T(8,128)}, u32[]{:S(2)}) copy-start(f32[2,64,8]{1,2,0:T(8,128)} %param.19) | copy-start | bytes 12292
  261.1 6.2 %copy-start.8 = (s32[2,64]{1,0:T(2,128)S(1)}, s32[2,64]{1,0:T(2,128)}, u32[]{:S(2)}) copy-start(s32[2,64]{1,0:T(2,128)} %param.18) | copy-start | bytes 1540
  261.1 11.4 %copy-start.2 = (bf16[2,64,2048]{2,1,0:T(8,128)(2,1)S(1)}, bf16[2,64,2048]{2,1,0:T(8,128)(2,1)}, u32[]{:S(2)}) copy-start(bf16[2,64,2048]{2,1,0:T(8,128)(2,1)} %param.10) | copy-start | bytes 1572868
  261.1 146.6 %all-to-all-start.1 = ((bf16[16,86,2048]{2,1,0:T(8,128)(2,1)}), bf16[16,86,2048]{2,1,0:T(8,128)(2,1)}, u32[]{:S(2)}, u32[]{:S(2)}) async-start(bf16[16,86,2048]{2,1,0:T(8,128)(2,1)} %reshape.257), calls=%async_computation.1 | async-start | bytes 11534336 | tf_op jit(solution)/shard_map/all_to_all | solution.py:51
  433.5 3.9 copy-start.3
  433.5 6.5 %copy-start.1 = (bf16[1,768,2048]{2,1,0:T(8,128)(2,1)S(1)}, bf16[1,768,2048]{2,1,0:T(8,128)(2,1)}, u32[]{:S(2)}) copy-start(bf16[1,768,2048]{2,1,0:T(8,128)(2,1)} %param.13) | copy-start | bytes 9437188
  437.5 1.6 copy-start.5
  437.5 1.6 slice-start
Sparse Core Ops, SparseCore 0:
  9.6 98.5 all-gather.3
  110.5 110.7 all-gather.5
  223.6 100.7 all-gather.7
where the time goes:
time: 447 us
  waiting for transfers between devices  302 us (68%)
  local copies, waits for them, and re-layouts  64.5 us (14%)
  matrix products  31.7 us (7%)
  other arithmetic  22.5 us (5%)
  between operations  13.5 us (3%)
  starting transfers between devices  12.2 us (3%)
    all_to_all x1, waiting for transfers between devices, shards(): lax.all_to_all(joined, 'expert', split_axis=0, concat_axis=0, tiled=True)  180 us
    all_to_all x1, waiting for transfers between devices, shards(): lax.all_to_all(expert_rows(lax.all_to_all(joined, 'expert', split_axis=0,...  73.7 us
    all_gather x1, waiting for transfers between devices, shards(): lax.all_gather(hot_down, 'expert', axis=2, tiled=True)  46.1 us
    gather x4, local copies, waits for them, and re-layouts, shards(): rows_out = tokens[micro][source // picks]  19.1 us
  transfers between devices with their start and end apart: 5, of which 3 were waited for; matrix products, arithmetic and copies ran while one was open for 19% of the time, Pallas kernels for 0%

commit v1 on v0

v1 whole, which is shorter than its diff:
```python
import jax
import jax.numpy as jnp
from jax import lax
from jax.sharding import PartitionSpec as P


def coefficients(cold_routes, hot_pick, gates, width, hot):
    cold = cold_routes[:, :, None] == jnp.arange(width, dtype=jnp.int32)
    cold = jnp.sum(jnp.where(cold, gates[:, 1:, None], 0.0), axis=1)
    warm = hot_pick[:, None] == jnp.arange(hot, dtype=jnp.int32)
    warm = jnp.where(warm, gates[:, :1], 0.0)
    return jnp.concatenate([cold, warm], axis=1).T


def shards(tokens, w_gate, w_up, w_down, hot_gate, hot_up, hot_down, cold_routes, hot_pick, gates):
    width = lax.axis_size("expert")
    me = lax.axis_index("expert")
    micro_count, local_tokens, model = tokens.shape
    hot = hot_gate.shape[0]
    units = w_gate.shape[2]
    part = hot_gate.shape[2]

    gate_w = jnp.concatenate([w_gate[0]] + [hot_gate[h] for h in range(hot)], axis=1)
    up_w = jnp.concatenate([w_up[0]] + [hot_up[h] for h in range(hot)], axis=1)
    down_w = jnp.concatenate([w_down[0]] + [hot_down[h].T for h in range(hot)], axis=0)

    table = coefficients(
        cold_routes.reshape(micro_count * local_tokens, -1),
        hot_pick.reshape(-1),
        gates.reshape(micro_count * local_tokens, -1),
        width,
        hot,
    )
    table = lax.all_gather(table, "expert", axis=0)
    cold_c = lax.dynamic_index_in_dim(table, me, axis=1, keepdims=False)
    hot_c = table[:, width:]

    outs = []
    for micro in range(micro_count):
        rows = lax.all_gather(tokens[micro], "expert", axis=0, tiled=True)
        span = slice(micro * local_tokens, (micro + 1) * local_tokens)
        scale = [jnp.broadcast_to(cold_c[:, span].reshape(-1, 1), (width * local_tokens, units))]
        for h in range(hot):
            scale.append(
                jnp.broadcast_to(hot_c[:, h, span].reshape(-1, 1), (width * local_tokens, part))
            )
        scale = jnp.concatenate(scale, axis=1)
        gate = jnp.dot(rows, gate_w, preferred_element_type=jnp.float32)
        upward = jnp.dot(rows, up_w, preferred_element_type=jnp.float32)
        hidden = (jax.nn.silu(gate) * upward * scale).astype(jnp.bfloat16)
        mixed = jnp.dot(hidden, down_w, preferred_element_type=jnp.float32).astype(jnp.bfloat16)
        outs.append(lax.psum_scatter(mixed, "expert", scatter_dimension=0, tiled=True))
    return jnp.stack(outs)


def solution(mesh):
    in_specs = (
        P(None, ("groups", "expert"), None),
        P("expert", None, None),
        P("expert", None, None),
        P("expert", None, None),
        P(None, None, "expert"),
        P(None, None, "expert"),
        P(None, None, "expert"),
        P(None, ("groups", "expert"), None),
        P(None, ("groups", "expert")),
        P(None, ("groups", "expert"), None),
    )
    out_specs = P(None, ("groups", "expert"), None)
    return jax.shard_map(shards, mesh=mesh, in_specs=in_specs, out_specs=out_specs, check_vma=False)
```

time: 447 us -> 274 us (0.61)
  the two profiles are of different devices: /device:TPU:13 before, /device:TPU:0 now
where the time goes in v1:
time: 274 us; the launch traced here: 273 us
  waiting for transfers between devices  168 us (61%)
  matrix products  52.6 us (19%)
  blocking collectives  23.9 us (9%)
  between operations  13.3 us (5%)
  local copies, waits for them, and re-layouts  13.1 us (5%)
    reduce_scatter x2, waiting for transfers between devices, shards(): lax.psum_scatter(mixed, 'expert', scatter_dimension=0, tiled=True)  124 us
    all_gather x2, waiting for transfers between devices, shards(): rows = lax.all_gather(tokens[micro], 'expert', axis=0, tiled=True)  43.9 us
    dot_general x2, matrix products, shards(): jnp.dot(hidden, down_w, preferred_element_type=jnp.float32)  34.2 us
    all_gather x1, blocking collectives, shards(): table = lax.all_gather(table, 'expert', axis=0)  23.9 us
    dot_general x2, matrix products, shards(): upward = jnp.dot(rows, up_w, preferred_element_type=jnp.float32)  18.4 us
  transfers between devices with their start and end apart: 4, of which 4 were waited for; matrix products, arithmetic and copies ran while one was open for 23% of the time, Pallas kernels for 0%

profile of v1, /device:TPU:0, one launch (start us, length us, event | category | flops | bytes accessed | tf_op | source)
XLA Modules:
  0.0 273.2 jit_solution(4734304952042405849)
XLA Ops:
  6.5 2.0 fusion.34
  8.6 0.7 all-gather.9.cloned.1.call-update
  9.3 0.7 copy.36
  10.1 0.1 reshape.14
  10.1 0.8 eq.30
  10.9 0.8 eq.34
  11.7 23.9 %all-gather.3 = f32[16,18,128]{2,1,0:T(8,128)S(1)} all-gather(f32[1,18,128]{2,1,0:T(8,128)S(1)} %maximum_bitcast_fusion), channel_id=3, replica_groups=mesh['groups'=2,'expert'=16] {'expert'}, dimensions={0}, use_global_device_ids=true | all-gather | bytes 156672 | tf_op jit(solution)/shard_map/all_gather | solution.py:34
  35.6 0.1 fusion.35
  35.7 0.7 broadcast_in_dim.76
  36.4 1.0 slice_bitcast_fusion.3
  37.4 0.3 copy.34
  37.7 0.3 copy.35
  38.0 0.8 slice_reduce_fusion.3
  38.7 0.7 broadcast_in_dim.78
  39.4 0.7 broadcast_in_dim.80
  40.1 1.0 copy.32
  41.1 1.0 copy.33
  42.1 0.8 slice_bitcast_fusion.1
  42.9 20.1 %all-gather.7.cloned.1.call-done = bf16[1,1024,2048]{2,1,0:T(8,128)(2,1)} async-done(((bf16[1,64,2048]{2,1,0:T(8,128)(2,1)}), bf16[1,1024,2048]{2,1,0:T(8,128)(2,1)}) %all-gather.7.cloned.1.call-update) | async-done | bytes 4194320 | tf_op jit(solution)/shard_map/all_gather | solution.py:40
  63.0 9.2 %fusion.4 = f32[864,1024]{1,0:T(8,128)} fusion(bf16[1,1024,2048]{2,1,0:T(8,128)(2,1)} %all-gather.7.cloned.1.call-done, bf16[2048,48]{1,0:T(8,128)(2,1)S(1)} %copy.35, bf16[2048,48]{1,0:T(8,128)(2,1)S(1)} %copy.34, bf16[2048,768]{1,0:T(8,128)(2,1)} %bitcast.97), kind=kOutput, calls=%fused_computation.4 | convolution fusion | flops 3634495488 | bytes 11272192 | tf_op jit(solution)/shard_map/dot_general | solution.py:49
  72.3 0.4 broadcast_in_dim.77
  72.7 16.8 %convolution_convert_fusion.1 = bf16[1024,2048]{1,0:T(8,128)(2,1)} fusion(f32[1024,48]{0,1:T(8,128)S(1)} %broadcast_in_dim.81, f32[1024,48]{0,1:T(8,128)S(1)} %broadcast_in_dim.79, f32[1024,768]{0,1:T(8,128)S(1)} %broadcast_in_dim.77, f32[864,1024]{1,0:T(8,128)} %fusion.4, bf16[1,1024,2048]{2,1,0:T(8,128)(2,1)} %all-gather.7.cloned.1.call-done, ...), kind=kOutput, calls=%fused_computation.9 | convolution fusion | flops 7279050752 | bytes 22544384 | tf_op jit(solution)/shard_map/dot_general | solution.py:51
  89.6 0.1 broadcast_in_dim.82
  89.7 0.5 copy-done.6
  90.2 0.1 broadcast_in_dim.84
  90.4 23.8 %all-gather.9.cloned.1.call-done = bf16[1,1024,2048]{2,1,0:T(8,128)(2,1)} async-done(((bf16[1,64,2048]{2,1,0:T(8,128)(2,1)}), bf16[1,1024,2048]{2,1,0:T(8,128)(2,1)}) %all-gather.9.cloned.1.call-update) | async-done | bytes 4194320 | tf_op jit(solution)/shard_map/all_gather | solution.py:40
  114.1 9.2 %fusion = f32[864,1024]{1,0:T(8,128)} fusion(bf16[1,1024,2048]{2,1,0:T(8,128)(2,1)} %all-gather.9.cloned.1.call-done, bf16[2048,48]{1,0:T(8,128)(2,1)S(1)} %copy-done.3, bf16[2048,48]{1,0:T(8,128)(2,1)S(1)} %copy-done.1, bf16[2048,768]{1,0:T(8,128)(2,1)} %bitcast.98), kind=kOutput, calls=%fused_computation | convolution fusion | flops 3634495488 | bytes 11272192 | tf_op jit(solution)/shard_map/dot_general | solution.py:49
  123.3 0.4 broadcast_in_dim.83
  123.8 17.4 %convolution_convert_fusion = bf16[1024,2048]{1,0:T(8,128)(2,1)} fusion(f32[1024,48]{0,1:T(8,128)S(1)} %broadcast_in_dim.87, f32[1024,48]{0,1:T(8,128)S(1)} %broadcast_in_dim.85, f32[1024,768]{0,1:T(8,128)S(1)} %broadcast_in_dim.83, f32[864,1024]{1,0:T(8,128)} %fusion, bf16[1,1024,2048]{2,1,0:T(8,128)(2,1)} %all-gather.9.cloned.1.call-done, ...), kind=kOutput, calls=%fused_computation.8 | convolution fusion | flops 7279050752 | bytes 22544384 | tf_op jit(solution)/shard_map/dot_general | solution.py:51
  141.2 48.1 %reduce-scatter.3.cloned.1.call-done = bf16[64,2048]{1,0:T(8,128)(2,1)} async-done(((bf16[1024,2048]{1,0:T(8,128)(2,1)}), bf16[64,2048]{1,0:T(8,128)(2,1)}) %reduce-scatter.3.cloned.1.call-update) | async-done | bytes 262160 | tf_op jit(solution)/shard_map/reduce_scatter | solution.py:52
  189.3 75.5 %reduce-scatter.5.cloned.1.call-done = bf16[64,2048]{1,0:T(8,128)(2,1)} async-done(((bf16[1024,2048]{1,0:T(8,128)(2,1)}), bf16[64,2048]{1,0:T(8,128)(2,1)}) %reduce-scatter.5.cloned.1.call-update) | async-done | bytes 262160 | tf_op jit(solution)/shard_map/reduce_scatter | solution.py:52
  264.8 1.9 pad_maximum_fusion.11
  (38 shorter events, 0.4 us)
Async XLA Ops:
  6.5 33.5 %copy-start.4 = (bf16[2,2048,48]{1,2,0:T(8,128)(2,1)S(1)}, bf16[2,2048,48]{1,2,0:T(8,128)(2,1)}, u32[]{:S(2)}) copy-start(bf16[2,2048,48]{1,2,0:T(8,128)(2,1)} %param.14) | copy-start | bytes 1179652
  6.5 35.6 %copy-start.5 = (bf16[2,2048,48]{1,2,0:T(8,128)(2,1)S(1)}, bf16[2,2048,48]{1,2,0:T(8,128)(2,1)}, u32[]{:S(2)}) copy-start(bf16[2,2048,48]{1,2,0:T(8,128)(2,1)} %param.16) | copy-start | bytes 1179652
  6.5 56.5 %all-gather.7.cloned.1.call-start = ((), (), s32[]{:S(2)}) async-start(), calls=%async_computation.4 | async-start | bytes 4456448 | tf_op jit(solution)/shard_map/all_gather | solution.py:40
  8.5 105.6 %all-gather.9.cloned.1.call-start = ((), (), s32[]{:S(2)}) async-start(), calls=%async_computation.5 | async-start | bytes 4456448 | tf_op jit(solution)/shard_map/all_gather | solution.py:40
  9.3 180.0 %reduce-scatter.3.cloned.1.call-start = ((), (), s32[]{:S(2)}) async-start(), calls=%async_computation.2 | async-start | bytes 4456448 | tf_op jit(solution)/shard_map/reduce_scatter | solution.py:52
  37.7 25.3 %copy-start = (bf16[2048,48]{1,0:T(8,128)(2,1)}, bf16[2048,48]{1,0:T(8,128)(2,1)S(1)}, u32[]{:S(2)}) copy-start(bf16[2048,48]{1,0:T(8,128)(2,1)S(1)} %copy.34) | copy-start | bytes 589828
  38.0 25.1 %copy-start.2 = (bf16[2048,48]{1,0:T(8,128)(2,1)}, bf16[2048,48]{1,0:T(8,128)(2,1)S(1)}, u32[]{:S(2)}) copy-start(bf16[2048,48]{1,0:T(8,128)(2,1)S(1)} %copy.35) | copy-start | bytes 589828
  63.0 9.2 %copy-start.7 = (f32[1024]{0:T(1024)S(1)}, f32[1024]{0:T(1024)}, u32[]{:S(2)}) copy-start(f32[1024]{0:T(1024)} %broadcast_in_dim.76) | copy-start | bytes 12292
  63.0 9.6 %copy-start.8 = (f32[1024]{0:T(1024)S(1)}, f32[1024]{0:T(1024)}, u32[]{:S(2)}) copy-start(f32[1024]{0:T(1024)} %broadcast_in_dim.78) | copy-start | bytes 12292
  63.0 9.7 %copy-start.9 = (f32[1024]{0:T(1024)S(1)}, f32[1024]{0:T(1024)}, u32[]{:S(2)}) copy-start(f32[1024]{0:T(1024)} %broadcast_in_dim.80) | copy-start | bytes 12292
  89.5 0.7 copy-start.6
  89.5 24.6 %copy-start.1 = (bf16[2048,48]{1,0:T(8,128)(2,1)S(1)}, bf16[2048,48]{1,0:T(8,128)(2,1)}, u32[]{:S(2)}) copy-start(bf16[2048,48]{1,0:T(8,128)(2,1)} %copy-done) | copy-start | bytes 589828
  89.5 24.6 %copy-start.3 = (bf16[2048,48]{1,0:T(8,128)(2,1)S(1)}, bf16[2048,48]{1,0:T(8,128)(2,1)}, u32[]{:S(2)}) copy-start(bf16[2048,48]{1,0:T(8,128)(2,1)} %copy-done.2) | copy-start | bytes 589828
  89.5 175.3 %reduce-scatter.5.cloned.1.call-start = ((), (), s32[]{:S(2)}) async-start(), calls=%async_computation.3 | async-start | bytes 4456448 | tf_op jit(solution)/shard_map/reduce_scatter | solution.py:52
Sparse Core Ops, SparseCore 0:
  9.5 53.4 all-gather.6
  65.2 48.8 all-gather.8
  118.0 71.2 reduce-scatter.2
  193.0 71.7 reduce-scatter.4

commit v2 on v0

--- a/solution.py
+++ b/solution.py
@@ -1,6 +1,10 @@
+import functools
+
 import jax
 import jax.numpy as jnp
 from jax import lax
+from jax.experimental import pallas as pl
+from jax.experimental.pallas import tpu as pltpu
 from jax.sharding import PartitionSpec as P
 
 TOP = 8
@@ -33,7 +37,7 @@
     return (slot_place, source, filled)
 
 
-def shards(tokens, w_gate, w_up, w_down, hot_gate, hot_up, hot_down, cold_routes, hot_pick, gates):
+def routed(tokens, w_gate, w_up, w_down, hot_gate, hot_up, hot_down, cold_routes, hot_pick, gates):
     axis_width = lax.axis_size("expert")
     micro_count, local_tokens, model_width = tokens.shape
     picks = TOP - 1
@@ -97,6 +101,383 @@
     return total.astype(jnp.bfloat16)
 
 
+QUARTERS = 4
+ROOM = 56 * 2**20
+
+
+def column(row):
+    rows = row.shape[1]
+    down = lax.broadcasted_iota(jnp.int32, (rows, rows), 0)
+    across = lax.broadcasted_iota(jnp.int32, (rows, rows), 1)
+    return jnp.sum(jnp.where(down == across, row, 0.0), axis=1, keepdims=True)
+
+
+def fused(
+    n, hot, part, tok, ct, wg_in, wu_in, wd_in, wh_in, out,
+    xs, keep, sc, rc, sy, ry, sz, rz, wg, wu, wd, wh, hid, hhid, cs,
+    wsem, tsem, cts, ctr, up_s, down_s, z_r, y_s, y_r, c_s, c_r,
+    rc_s, rc_r, ry_s, ry_r, rz_s, rz_r,
+):
+    nz = n // 4
+    rows, model = tok.shape
+    units = wg.shape[1]
+    pad = hhid.shape[1]
+    piece = rows // QUARTERS
+    me = lax.axis_index("expert")
+    c = lax.rem(me, 2)
+    y = lax.rem(lax.div(me, 2), 2)
+    z = lax.div(me, 4)
+    own = y * 2 + c
+    side = (1 - y) * 2 + c
+    peer_y = z * 4 + side
+    peer_c = z * 4 + y * 2 + (1 - c)
+
+    def remote(src, dst, send, recv, device):
+        return pltpu.make_async_remote_copy(
+            src_ref=src, dst_ref=dst, send_sem=send, recv_sem=recv,
+            device_id={"expert": device}, device_id_type=pl.DeviceIdType.MESH,
+        )
+
+    loads = [
+        pltpu.make_async_copy(src, dst, wsem.at[i])
+        for i, (src, dst) in enumerate(((wg_in, wg), (wu_in, wu), (wd_in, wd), (wh_in, wh)))
+    ]
+    first = pltpu.make_async_copy(tok, xs.at[z, own], tsem)
+    first.start()
+    for load in loads:
+        load.start()
+
+    barrier = pltpu.get_barrier_semaphore()
+
+    @pl.loop(1, n)
+    def _(i):
+        pl.semaphore_signal(
+            barrier, inc=1, device_id={"expert": lax.rem(me + i, n)},
+            device_id_type=pl.DeviceIdType.MESH,
+        )
+
+    pl.semaphore_wait(barrier, n - 1)
+
+    def ct_copy(i):
+        peer = lax.rem(me + i, n)
+        return remote(ct.at[peer], cs.at[me], cts.at[i], ctr.at[me], peer)
+
+    def go_up(p):
+        return remote(xs.at[p, own], xs.at[p, own], up_s.at[p], z_r.at[p], me + 4)
+
+    def go_down(p):
+        return remote(xs.at[p, own], xs.at[p, own], down_s.at[p], z_r.at[p], me - 4)
+
+    def go_y(p):
+        return remote(xs.at[p, own], xs.at[p, own], y_s.at[p], y_r.at[p], peer_y)
+
+    def go_c(p, which):
+        slot = own if which == 0 else side
+        return remote(
+            xs.at[p, slot], xs.at[p, slot], c_s.at[p, which], c_r.at[p, which], peer_c
+        )
+
+    def spread(p):
+        @pl.when((p <= z) & (z + 1 < nz))
+        def _():
+            go_up(p).start()
+
+        @pl.when((p >= z) & (z > 0))
+        def _():
+            go_down(p).start()
+
+        go_y(p).start()
+        go_c(p, 0).start()
+
+    def landed(p):
+        remote(xs.at[p, own], xs.at[p, own], up_s.at[p], z_r.at[p], me).wait_recv()
+        spread(p)
+
+    def plane(s):
+        near = jnp.minimum(z, nz - 1 - z)
+        step = lax.div(s + 1, 2)
+        both = jnp.where(lax.rem(s, 2) == 1, z - step, z + step)
+        far = jnp.where(z * 2 < nz, s, nz - 1 - s)
+        return jnp.where(s <= 2 * near, both, far)
+
+    def share(p, j, q):
+        span = pl.ds(pl.multiple_of(q * piece, piece), piece)
+        return remote(
+            sc.at[p, j, span], rc.at[p, j, span], rc_s.at[p, j, q], rc_r.at[p, j, q], peer_c
+        )
+
+    def share_y(p, q):
+        span = pl.ds(pl.multiple_of(q * piece, piece), piece)
+        return remote(sy.at[p, span], ry.at[p, span], ry_s.at[p, q], ry_r.at[p, q], peer_y)
+
+    def share_z(way, p, q):
+        span = pl.ds(pl.multiple_of(q * piece, piece), piece)
+        return remote(
+            sz.at[way, p, span], rz.at[way, p, span], rz_s.at[way, p, q], rz_r.at[way, p, q],
+            jnp.where(way == 0, me + 4, me - 4),
+        )
+
+    def compute(p):
+        wide = 256 if units % 256 == 0 else units
+        x = xs.at[p]
+        cold_c = jnp.concatenate([column(cs[p * 4 + j, 0:1, :]) for j in range(4)], axis=0)
+
+        @pl.loop(0, units // wide)
+        def _(k):
+            cols = pl.ds(pl.multiple_of(k * wide, wide), wide)
+            v = x[...].reshape(4 * rows, model)
+            g = jnp.dot(v, wg[:, cols], preferred_element_type=jnp.float32)
+            u = jnp.dot(v, wu[:, cols], preferred_element_type=jnp.float32)
+            hid[:, cols] = (g / (1.0 + jnp.exp(-g)) * u).astype(jnp.bfloat16)
+
+        v = x[...].reshape(4 * rows, model)
+        gu = jnp.dot(v, wh[:, : 2 * pad], preferred_element_type=jnp.float32)
+        g, u = gu[:, :pad], gu[:, pad:]
+        lane = lax.broadcasted_iota(jnp.int32, (rows, pad), 1)
+        warm = []
+        for j in range(4):
+            scale = jnp.zeros((rows, pad), jnp.float32)
+            for h in range(hot):
+                weight = column(cs[p * 4 + j, 1 + h : 2 + h, :])
+                scale = jnp.where((lane >= h * part) & (lane < (h + 1) * part), weight, scale)
+            warm.append(scale)
+        warm = jnp.concatenate(warm, axis=0)
+        hhid[...] = (g / (1.0 + jnp.exp(-g)) * u * warm).astype(jnp.bfloat16)
+
+        tile = 512 if model % 512 == 0 else model
+
+        @pl.loop(0, model // tile)
+        def _(k):
+            cols = pl.ds(pl.multiple_of(k * tile, tile), tile)
+            r = jnp.dot(hid[...], wd[:, cols], preferred_element_type=jnp.float32)
+            r = r.astype(jnp.bfloat16).astype(jnp.float32) * cold_c
+            r = r + lax.dot_general(
+                hhid[...], wh[cols, 2 * pad :], (((1,), (1,)), ((), ())),
+                preferred_element_type=jnp.float32,
+            )
+            for j in range(2):
+                low = r[2 * j * rows : (2 * j + 1) * rows]
+                high = r[(2 * j + 1) * rows : (2 * j + 2) * rows]
+                keep[p, j, :, cols] = jnp.where(c == 0, low, high)
+                sc[p, j, :, cols] = jnp.where(c == 0, high, low).astype(jnp.bfloat16)
+
+    def y_step(p):
+        @pl.loop(0, QUARTERS)
+        def _(q):
+            span = pl.ds(pl.multiple_of(q * piece, piece), piece)
+            share(p, 1 - y, q).wait_recv()
+            total = keep[p, 1 - y, span, :] + rc[p, 1 - y, span, :].astype(jnp.float32)
+            sy[p, span, :] = total.astype(jnp.bfloat16)
+            share_y(p, q).start()
+
+        @pl.loop(0, QUARTERS)
+        def _(q):
+            span = pl.ds(pl.multiple_of(q * piece, piece), piece)
+            share(p, y, q).wait_recv()
+            keep[p, y, span, :] += rc[p, y, span, :].astype(jnp.float32)
+
+    def z_step(k):
+        @pl.loop(0, 2)
+        def _(turn):
+            way = jnp.where(z * 2 < nz, turn, 1 - turn)
+            p = jnp.where(way == 0, k, nz - 1 - k)
+            active = jnp.where(way == 0, z < k, z > nz - 1 - k)
+            fed = jnp.where(way == 0, z > 0, z < nz - 1)
+
+            @pl.when(active)
+            def _():
+                @pl.loop(0, QUARTERS)
+                def _(q):
+                    span = pl.ds(pl.multiple_of(q * piece, piece), piece)
+                    share_y(p, q).wait_recv()
+                    keep[p, y, span, :] += ry[p, span, :].astype(jnp.float32)
+
+                    @pl.when(fed)
+                    def _():
+                        share_z(way, p, q).wait_recv()
+                        keep[p, y, span, :] += rz[way, p, span, :].astype(jnp.float32)
+
+                    sz[way, p, span, :] = keep[p, y, span, :].astype(jnp.bfloat16)
+                    share_z(way, p, q).start()
+
+    first.wait()
+    spread(z)
+
+    @pl.loop(1, n)
+    def _(i):
+        ct_copy(i).start()
+
+    cs[me] = ct[me]
+
+    @pl.loop(0, nz)
+    def _(s):
+        p = plane(s)
+
+        @pl.when((s + 1 < nz) & (z - s - 1 >= 0))
+        def _():
+            landed(z - s - 1)
+
+        @pl.when((s + 1 < nz) & (z + s + 1 < nz))
+        def _():
+            landed(z + s + 1)
+
+        go_y(p).wait_recv()
+        go_c(p, 1).start()
+
+        @pl.when(s == 0)
+        def _():
+            for load in loads:
+                load.wait()
+
+            @pl.loop(1, n)
+            def _(i):
+                other = lax.rem(me + i, n)
+                remote(ct.at[other], cs.at[other], cts.at[i], ctr.at[other], other).wait_recv()
+
+        go_c(p, 0).wait_recv()
+        go_c(p, 1).wait_recv()
+        compute(p)
+
+        @pl.loop(0, QUARTERS)
+        def _(q):
+            share(p, 1 - y, q).start()
+
+        @pl.loop(0, QUARTERS)
+        def _(q):
+            share(p, y, q).start()
+
+        @pl.when(s >= 1)
+        def _():
+            y_step(plane(s - 1))
+
+        @pl.when(s >= 3)
+        def _():
+            z_step(s - 2)
+
+    y_step(plane(nz - 1))
+    for k in range(max(1, nz - 2), nz):
+        z_step(k)
+
+    @pl.loop(0, QUARTERS)
+    def _(q):
+        span = pl.ds(pl.multiple_of(q * piece, piece), piece)
+        share_y(z, q).wait_recv()
+        keep[z, y, span, :] += ry[z, span, :].astype(jnp.float32)
+
+        @pl.when(z > 0)
+        def _():
+            share_z(0, z, q).wait_recv()
+            keep[z, y, span, :] += rz[0, z, span, :].astype(jnp.float32)
+
+        @pl.when(z < nz - 1)
+        def _():
+            share_z(1, z, q).wait_recv()
+            keep[z, y, span, :] += rz[1, z, span, :].astype(jnp.float32)
+
+        out[span, :] = keep[z, y, span, :].astype(jnp.bfloat16)
+
+    @pl.loop(1, n)
+    def _(i):
+        ct_copy(i).wait_send()
+
+    @pl.loop(0, nz)
+    def _(p):
+        @pl.when((p <= z) & (z + 1 < nz))
+        def _():
+            go_up(p).wait_send()
+
+        @pl.when((p >= z) & (z > 0))
+        def _():
+            go_down(p).wait_send()
+
+        go_y(p).wait_send()
+        go_c(p, 0).wait_send()
+        go_c(p, 1).wait_send()
+
+        @pl.loop(0, QUARTERS)
+        def _(q):
+            share(p, 0, q).wait_send()
+            share(p, 1, q).wait_send()
+            share_y(p, q).wait_send()
+
+            @pl.when(p > z)
+            def _():
+                share_z(0, p, q).wait_send()
+
+            @pl.when(p < z)
+            def _():
+                share_z(1, p, q).wait_send()
+
+
+def scratch(n, rows, model, units, pad):
+    nz = n // 4
+    half, full = jnp.bfloat16, jnp.float32
+    dma = pltpu.SemaphoreType.DMA
+    return [
+        pltpu.VMEM((nz, 4, rows, model), half),
+        pltpu.VMEM((nz, 2, rows, model), full),
+        pltpu.VMEM((nz, 2, rows, model), half),
+        pltpu.VMEM((nz, 2, rows, model), half),
+        pltpu.VMEM((nz, rows, model), half),
+        pltpu.VMEM((nz, rows, model), half),
+        pltpu.VMEM((2, nz, rows, model), half),
+        pltpu.VMEM((2, nz, rows, model), half),
+        pltpu.VMEM((model, units), half),
+        pltpu.VMEM((model, units), half),
+        pltpu.VMEM((units, model), half),
+        pltpu.VMEM((model, 3 * pad), half),
+        pltpu.VMEM((4 * rows, units), half),
+        pltpu.VMEM((4 * rows, pad), half),
+        pltpu.VMEM((n, 8, rows), full),
+        dma((4,)), dma, dma((n,)), dma((n,)),
+        dma((nz,)), dma((nz,)), dma((nz,)), dma((nz,)), dma((nz,)), dma((nz, 2)), dma((nz, 2)),
+        dma((nz, 2, QUARTERS)), dma((nz, 2, QUARTERS)),
+        dma((nz, QUARTERS)), dma((nz, QUARTERS)),
+        dma((2, nz, QUARTERS)), dma((2, nz, QUARTERS)),
+    ]
+
+
+def shards(tokens, w_gate, w_up, w_down, hot_gate, hot_up, hot_down, cold_routes, hot_pick, gates):
+    n = lax.axis_size("expert")
+    micro_count, local_tokens, model = tokens.shape
+    rows = micro_count * local_tokens
+    hot, units, part = hot_gate.shape[0], w_gate.shape[2], hot_gate.shape[2]
+    pad = -(-hot * part // 128) * 128
+    need = rows * model * n * 9 // 2 * 2 + 3 * model * (units + pad) * 2
+    if n % 4 or rows % 64 or need > ROOM or hot > 7:
+        return routed(
+            tokens, w_gate, w_up, w_down, hot_gate, hot_up, hot_down, cold_routes, hot_pick, gates
+        )
+    routes = cold_routes.reshape(rows, -1).T
+    weights = gates.reshape(rows, -1).T
+    chosen = routes[None] == jnp.arange(n, dtype=jnp.int32)[:, None, None]
+    cold = jnp.sum(jnp.where(chosen, weights[None, 1:], 0.0), axis=1)
+    warm = hot_pick.reshape(1, rows) == jnp.arange(hot, dtype=jnp.int32)[:, None]
+    warm = jnp.where(warm, weights[:1], 0.0)
+    table = jnp.concatenate(
+        [cold[:, None], jnp.broadcast_to(warm[None], (n, hot, rows)),
+         jnp.zeros((n, 7 - hot, rows), jnp.float32)], axis=1,
+    )
+    blank = [jnp.zeros((model, pad - hot * part), jnp.bfloat16)] if pad > hot * part else []
+    joined = jnp.concatenate(
+        [v for w in (hot_gate, hot_up, hot_down) for v in [w[h] for h in range(hot)] + blank],
+        axis=1,
+    )
+    anyplace = pl.BlockSpec(memory_space=pl.ANY)
+    vmem = pl.BlockSpec(memory_space=pltpu.VMEM)
+    mixed = pl.pallas_call(
+        functools.partial(fused, n, hot, part),
+        out_shape=jax.ShapeDtypeStruct((rows, model), jnp.bfloat16),
+        in_specs=[anyplace, vmem, anyplace, anyplace, anyplace, anyplace],
+        out_specs=vmem,
+        scratch_shapes=scratch(n, rows, model, units, pad),
+        compiler_params=pltpu.CompilerParams(
+            collective_id=0, has_side_effects=True, vmem_limit_bytes=64 * 2**20 - 2**17
+        ),
+    )(tokens.reshape(rows, model), table, w_gate[0], w_up[0], w_down[0], joined)
+    return mixed.reshape(tokens.shape)
+
+
 def solution(mesh):
     in_specs = (
         P(None, ("groups", "expert"), None),

time: 447 us -> 142 us (0.32)
  the two profiles are of different devices: /device:TPU:13 before, /device:TPU:0 now
where the time goes in v2:
time: 142 us
  Pallas kernels  128 us (90%)
  local copies, waits for them, and re-layouts  13.2 us (9%)
    pallas_call x1, Pallas kernels, shards(): pl.pallas_call(functools.partial(fused, n, hot, part), out_shape=jax.Shap...  128 us
    concatenate x1, local copies, waits for them, and re-layouts, shards(): jnp.concatenate([v for w in (hot_gate, hot_up, hot_down) for v in [w[h] f...  6.31 us
    unnamed x16, local copies, waits for them, and re-layouts  4.29 us

profile of v2, /device:TPU:0, one launch (start us, length us, event | category | flops | bytes accessed | tf_op | source)
XLA Modules:
  0.0 141.9 jit_solution(1548302080166797925)
XLA Ops:
  0.0 0.0 copy-start
  0.0 1.1 fusion.1
  1.1 0.3 copy.33
  1.4 0.3 copy.34
  1.7 1.1 fusion
  2.7 0.3 copy.35
  3.0 0.3 copy.36
  3.3 0.0 copy-done
  3.3 0.3 copy.31
  3.6 1.0 copy.32
  4.6 0.1 broadcast_in_dim.50
  4.7 0.0 copy-start.1
  4.7 0.0 copy-start.3
  4.7 0.0 copy-start.2
  4.7 6.3 %concatenate.7.wh_in = bf16[2048,384]{1,0:T(8,128)(2,1)} concatenate(bf16[2048,48]{1,0:T(8,128)(2,1)S(1)} %bitcast.27, bf16[2048,48]{1,0:T(8,128)(2,1)} %bitcast.28, bf16[2048,32]{1,0:T(8,128)(2,1)S(1)} %broadcast_in_dim.50, bf16[2048,48]{1,0:T(8,128)(2,1)S(1)} %bitcast.23, bf16[2048,48]{1,0:T(8,128)(2,1)S(1)} %bitcast.24, bf16[2048,32]{1,0:T(8,128)(2,1)S(1)} %broadcast_in_dim.50, ...), dimensions={1} | concatenate | bytes 3145728 | tf_op jit(solution)/shard_map/concatenate | solution.py:462
  11.0 0.0 copy-done.1
  11.0 0.1 reshape.58
  11.1 0.0 copy-done.3
  11.1 0.1 eq.35
  11.2 0.0 copy-done.2
  11.3 0.1 reshape.57
  11.4 0.1 pad.2.clone
  11.4 0.7 maximum_maximum_fusion.ct
  12.1 127.8 %shard_map.100 = bf16[128,2048]{1,0:T(8,128)(2,1)} custom-call(bf16[128,2048]{1,0:T(8,128)(2,1)} %bitcast.30, f32[16,8,128]{2,1,0:T(8,128)} %maximum_maximum_fusion.ct, bf16[2048,768]{1,0:T(8,128)(2,1)} %bitcast.20, bf16[2048,768]{1,0:T(8,128)(2,1)} %bitcast.21, bf16[768,2048]{1,0:T(8,128)(2,1)} %bitcast.22, bf16[2048,384]{1,0:T(8,128)(2,1)} %concatenate.7.wh_in), custom_call_target="tpu_custom_call" | custom-call | tf_op jit(solution)/shard_map/pallas_call | solution.py:468
  140.0 1.9 %copy.38 = bf16[2,64,2048]{2,1,0:T(8,128)(2,1)} copy(bf16[2,64,2048]{2,1,0:T(8,128)(2,1)} %bitcast.29) | data formatting | bytes 1048576
  (8 shorter events, 0.1 us)
Async XLA Ops:
  0.0 3.3 %copy-start = (bf16[2,2048,48]{1,2,0:T(8,128)(2,1)S(1)}, bf16[2,2048,48]{1,2,0:T(8,128)(2,1)}, u32[]{:S(2)}) copy-start(bf16[2,2048,48]{1,2,0:T(8,128)(2,1)} %param.14) | copy-start | bytes 1179652
  4.7 6.3 %copy-start.1 = (f32[2,64,8]{1,2,0:T(8,128)S(1)}, f32[2,64,8]{1,2,0:T(8,128)}, u32[]{:S(2)}) copy-start(f32[2,64,8]{1,2,0:T(8,128)} %param.19) | copy-start | bytes 12292
  4.7 6.4 %copy-start.3 = (s32[2,64]{1,0:T(2,128)S(1)}, s32[2,64]{1,0:T(2,128)}, u32[]{:S(2)}) copy-start(s32[2,64]{1,0:T(2,128)} %param.18) | copy-start | bytes 1540
  4.7 6.5 %copy-start.2 = (s32[2,64,7]{1,0,2:T(2,128)S(1)}, s32[2,64,7]{1,0,2:T(2,128)}, u32[]{:S(2)}) copy-start(s32[2,64,7]{1,0,2:T(2,128)} %param.17) | copy-start | bytes 10756

commit v3 on v2

--- a/solution.py
+++ b/solution.py
@@ -113,10 +113,10 @@
 
 
 def fused(
-    n, hot, part, tok, ct, wg_in, wu_in, wd_in, wh_in, out,
-    xs, keep, sc, rc, sy, ry, sz, rz, wg, wu, wd, wh, hid, hhid, cs,
+    n, hot, part, tok, routes, pick, gts, wg_in, wu_in, wd_in, hg_in, hu_in, hd_in, out,
+    xs, keep, sc, rc, sy, ry, sz, rz, wg, wu, wd, wh, hid, hhid, cs, ct, sze, rze,
     wsem, tsem, cts, ctr, up_s, down_s, z_r, y_s, y_r, c_s, c_r,
-    rc_s, rc_r, ry_s, ry_r, rz_s, rz_r,
+    rc_s, rc_r, ry_s, ry_r, rz_s, rz_r, eu_s, ed_s, e_r, ez_s, ez_r,
 ):
     nz = n // 4
     rows, model = tok.shape
@@ -140,7 +140,13 @@
 
     loads = [
         pltpu.make_async_copy(src, dst, wsem.at[i])
-        for i, (src, dst) in enumerate(((wg_in, wg), (wu_in, wu), (wd_in, wd), (wh_in, wh)))
+        for i, (src, dst) in enumerate((
+            *(
+                (src.at[h], wh.at[pl.ds(t * pad + h * part, part)])
+                for t, src in enumerate((hg_in, hu_in, hd_in)) for h in range(hot)
+            ),
+            (wg_in, wg), (wu_in, wu), (wd_in, wd),
+        ))
     ]
     first = pltpu.make_async_copy(tok, xs.at[z, own], tsem)
     first.start()
@@ -171,6 +177,27 @@
     def go_y(p):
         return remote(xs.at[p, own], xs.at[p, own], y_s.at[p], y_r.at[p], peer_y)
 
+    def rest_y(p):
+        rest = xs.at[p, own, pl.ds(piece, rows - piece)]
+        return remote(rest, rest, y_s.at[p], y_r.at[p], peer_y)
+
+    def edge(p, send, device):
+        lead = xs.at[p, side, pl.ds(0, piece)]
+        return remote(lead, lead, send.at[p], e_r.at[p], device)
+
+    def spread_edge(p):
+        @pl.when((p <= z) & (z + 1 < nz))
+        def _():
+            edge(p, eu_s, me + 4).start()
+
+        @pl.when((p >= z) & (z > 0))
+        def _():
+            edge(p, ed_s, me - 4).start()
+
+    def landed_edge(p):
+        edge(p, eu_s, me).wait_recv()
+        spread_edge(p)
+
     def go_c(p, which):
         slot = own if which == 0 else side
         return remote(
@@ -186,12 +213,11 @@
         def _():
             go_down(p).start()
 
-        go_y(p).start()
-        go_c(p, 0).start()
-
     def landed(p):
         remote(xs.at[p, own], xs.at[p, own], up_s.at[p], z_r.at[p], me).wait_recv()
         spread(p)
+        rest_y(p).start()
+        go_c(p, 0).start()
 
     def plane(s):
         near = jnp.minimum(z, nz - 1 - z)
@@ -231,7 +257,9 @@
             hid[:, cols] = (g / (1.0 + jnp.exp(-g)) * u).astype(jnp.bfloat16)
 
         v = x[...].reshape(4 * rows, model)
-        gu = jnp.dot(v, wh[:, : 2 * pad], preferred_element_type=jnp.float32)
+        gu = lax.dot_general(
+            v, wh[: 2 * pad, :], (((1,), (1,)), ((), ())), preferred_element_type=jnp.float32
+        )
         g, u = gu[:, :pad], gu[:, pad:]
         lane = lax.broadcasted_iota(jnp.int32, (rows, pad), 1)
         warm = []
@@ -251,10 +279,7 @@
             cols = pl.ds(pl.multiple_of(k * tile, tile), tile)
             r = jnp.dot(hid[...], wd[:, cols], preferred_element_type=jnp.float32)
             r = r.astype(jnp.bfloat16).astype(jnp.float32) * cold_c
-            r = r + lax.dot_general(
-                hhid[...], wh[cols, 2 * pad :], (((1,), (1,)), ((), ())),
-                preferred_element_type=jnp.float32,
-            )
+            r = r + jnp.dot(hhid[...], wh[2 * pad :, cols], preferred_element_type=jnp.float32)
             for j in range(2):
                 low = r[2 * j * rows : (2 * j + 1) * rows]
                 high = r[(2 * j + 1) * rows : (2 * j + 2) * rows]
@@ -262,7 +287,10 @@
                 sc[p, j, :, cols] = jnp.where(c == 0, high, low).astype(jnp.bfloat16)
 
     def y_step(p):
-        @pl.loop(0, QUARTERS)
+        share(p, 1 - y, 0).wait_recv()
+        keep[p, 1 - y, 0:piece, :] += rc[p, 1 - y, 0:piece, :].astype(jnp.float32)
+
+        @pl.loop(1, QUARTERS)
         def _(q):
             span = pl.ds(pl.multiple_of(q * piece, piece), piece)
             share(p, 1 - y, q).wait_recv()
@@ -275,6 +303,12 @@
             span = pl.ds(pl.multiple_of(q * piece, piece), piece)
             share(p, y, q).wait_recv()
             keep[p, y, span, :] += rc[p, y, span, :].astype(jnp.float32)
+
+    def share_edge(way, p):
+        return remote(
+            sze.at[way, p], rze.at[way, p], ez_s.at[way, p], ez_r.at[way, p],
+            jnp.where(way == 0, me + 4, me - 4),
+        )
 
     def z_step(k):
         @pl.loop(0, 2)
@@ -286,11 +320,22 @@
 
             @pl.when(active)
             def _():
+                @pl.when(fed)
+                def _():
+                    share_edge(way, p).wait_recv()
+                    keep[p, 1 - y, 0:piece, :] += rze[way, p].astype(jnp.float32)
+
+                sze[way, p] = keep[p, 1 - y, 0:piece, :].astype(jnp.bfloat16)
+                share_edge(way, p).start()
+
                 @pl.loop(0, QUARTERS)
                 def _(q):
                     span = pl.ds(pl.multiple_of(q * piece, piece), piece)
-                    share_y(p, q).wait_recv()
-                    keep[p, y, span, :] += ry[p, span, :].astype(jnp.float32)
+
+                    @pl.when(q > 0)
+                    def _():
+                        share_y(p, q).wait_recv()
+                        keep[p, y, span, :] += ry[p, span, :].astype(jnp.float32)
 
                     @pl.when(fed)
                     def _():
@@ -302,6 +347,37 @@
 
     first.wait()
     spread(z)
+    go_y(z).start()
+    go_c(z, 0).start()
+
+    if pad > hot * part:
+        for t in range(3):
+            blank = wh.at[pl.ds(t * pad + hot * part, pad - hot * part)]
+            blank[...] = jnp.zeros_like(blank)
+
+    ct[...] = jnp.zeros_like(ct)
+    micros = gts.shape[0]
+
+    def joined(parts):
+        return jnp.concatenate(parts, axis=1)
+
+    warm_row = joined([gts[m, 0:1, :] for m in range(micros)])
+    chosen = joined([pick[m : m + 1, :] for m in range(micros)])
+    named = [
+        (
+            joined([routes[k, m : m + 1, :] for m in range(micros)]),
+            joined([gts[m, k + 1 : k + 2, :] for m in range(micros)]),
+        )
+        for k in range(routes.shape[0])
+    ]
+
+    def row(e):
+        return sum(jnp.where(route == e, weight, 0.0) for route, weight in named)
+
+    for e in range(n):
+        ct[e, 0:1, :] = row(e)
+        for h in range(hot):
+            ct[e, 1 + h : 2 + h, :] = jnp.where(chosen == h, warm_row, 0.0)
 
     @pl.loop(1, n)
     def _(i):
@@ -321,7 +397,23 @@
         def _():
             landed(z + s + 1)
 
-        go_y(p).wait_recv()
+        @pl.when(s == 0)
+        def _():
+            go_y(z).wait_recv()
+            spread_edge(z)
+
+        @pl.when((s > 0) & (z - s >= 0))
+        def _():
+            landed_edge(z - s)
+
+        @pl.when((s > 0) & (z + s < nz))
+        def _():
+            landed_edge(z + s)
+
+        @pl.when(s > 0)
+        def _():
+            rest_y(p).wait_recv()
+
         go_c(p, 1).start()
 
         @pl.when(s == 0)
@@ -358,8 +450,24 @@
     for k in range(max(1, nz - 2), nz):
         z_step(k)
 
-    @pl.loop(0, QUARTERS)
-    def _(q):
+    lead = keep.at[z, 1 - y, pl.ds(0, piece)]
+
+    @pl.when(z > 0)
+    def _():
+        share_edge(0, z).wait_recv()
+        lead[...] += rze[0, z].astype(jnp.float32)
+
+    @pl.when(z < nz - 1)
+    def _():
+        share_edge(1, z).wait_recv()
+        lead[...] += rze[1, z].astype(jnp.float32)
+
+    sy[z, 0:piece, :] = lead[...].astype(jnp.bfloat16)
+    share_y(z, 0).start()
+
+    @pl.loop(1, QUARTERS + 1)
+    def _(turn):
+        q = lax.rem(turn, QUARTERS)
         span = pl.ds(pl.multiple_of(q * piece, piece), piece)
         share_y(z, q).wait_recv()
         keep[z, y, span, :] += ry[z, span, :].astype(jnp.float32)
@@ -390,7 +498,30 @@
         def _():
             go_down(p).wait_send()
 
-        go_y(p).wait_send()
+        @pl.when((p <= z) & (z + 1 < nz))
+        def _():
+            edge(p, eu_s, me + 4).wait_send()
+
+        @pl.when((p >= z) & (z > 0))
+        def _():
+            edge(p, ed_s, me - 4).wait_send()
+
+        @pl.when(p == z)
+        def _():
+            go_y(p).wait_send()
+
+        @pl.when(p != z)
+        def _():
+            rest_y(p).wait_send()
+
+        @pl.when(p > z)
+        def _():
+            share_edge(0, p).wait_send()
+
+        @pl.when(p < z)
+        def _():
+            share_edge(1, p).wait_send()
+
         go_c(p, 0).wait_send()
         go_c(p, 1).wait_send()
 
@@ -398,7 +529,10 @@
         def _(q):
             share(p, 0, q).wait_send()
             share(p, 1, q).wait_send()
-            share_y(p, q).wait_send()
+
+            @pl.when((q > 0) | (p == z))
+            def _():
+                share_y(p, q).wait_send()
 
             @pl.when(p > z)
             def _():
@@ -409,8 +543,9 @@
                 share_z(1, p, q).wait_send()
 
 
-def scratch(n, rows, model, units, pad):
+def scratch(n, rows, model, units, pad, hot):
     nz = n // 4
+    piece = rows // QUARTERS
     half, full = jnp.bfloat16, jnp.float32
     dma = pltpu.SemaphoreType.DMA
     return [
@@ -425,15 +560,19 @@
         pltpu.VMEM((model, units), half),
         pltpu.VMEM((model, units), half),
         pltpu.VMEM((units, model), half),
-        pltpu.VMEM((model, 3 * pad), half),
+        pltpu.VMEM((3 * pad, model), half),
         pltpu.VMEM((4 * rows, units), half),
         pltpu.VMEM((4 * rows, pad), half),
         pltpu.VMEM((n, 8, rows), full),
-        dma((4,)), dma, dma((n,)), dma((n,)),
+        pltpu.VMEM((n, 8, rows), full),
+        pltpu.VMEM((2, nz, piece, model), half),
+        pltpu.VMEM((2, nz, piece, model), half),
+        dma((3 + 3 * hot,)), dma, dma((n,)), dma((n,)),
         dma((nz,)), dma((nz,)), dma((nz,)), dma((nz,)), dma((nz,)), dma((nz, 2)), dma((nz, 2)),
         dma((nz, 2, QUARTERS)), dma((nz, 2, QUARTERS)),
         dma((nz, QUARTERS)), dma((nz, QUARTERS)),
         dma((2, nz, QUARTERS)), dma((2, nz, QUARTERS)),
+        dma((nz,)), dma((nz,)), dma((nz,)), dma((2, nz)), dma((2, nz)),
     ]
 
 
@@ -444,37 +583,27 @@
     hot, units, part = hot_gate.shape[0], w_gate.shape[2], hot_gate.shape[2]
     pad = -(-hot * part // 128) * 128
     need = rows * model * n * 9 // 2 * 2 + 3 * model * (units + pad) * 2
-    if n % 4 or rows % 64 or need > ROOM or hot > 7:
+    if n % 4 or part % 16 or rows % 64 or model % 256 or need > ROOM or hot > 7:
         return routed(
             tokens, w_gate, w_up, w_down, hot_gate, hot_up, hot_down, cold_routes, hot_pick, gates
         )
-    routes = cold_routes.reshape(rows, -1).T
-    weights = gates.reshape(rows, -1).T
-    chosen = routes[None] == jnp.arange(n, dtype=jnp.int32)[:, None, None]
-    cold = jnp.sum(jnp.where(chosen, weights[None, 1:], 0.0), axis=1)
-    warm = hot_pick.reshape(1, rows) == jnp.arange(hot, dtype=jnp.int32)[:, None]
-    warm = jnp.where(warm, weights[:1], 0.0)
-    table = jnp.concatenate(
-        [cold[:, None], jnp.broadcast_to(warm[None], (n, hot, rows)),
-         jnp.zeros((n, 7 - hot, rows), jnp.float32)], axis=1,
-    )
-    blank = [jnp.zeros((model, pad - hot * part), jnp.bfloat16)] if pad > hot * part else []
-    joined = jnp.concatenate(
-        [v for w in (hot_gate, hot_up, hot_down) for v in [w[h] for h in range(hot)] + blank],
-        axis=1,
-    )
     anyplace = pl.BlockSpec(memory_space=pl.ANY)
     vmem = pl.BlockSpec(memory_space=pltpu.VMEM)
     mixed = pl.pallas_call(
         functools.partial(fused, n, hot, part),
         out_shape=jax.ShapeDtypeStruct((rows, model), jnp.bfloat16),
-        in_specs=[anyplace, vmem, anyplace, anyplace, anyplace, anyplace],
+        in_specs=[anyplace, vmem, vmem, vmem] + [anyplace] * 6,
         out_specs=vmem,
-        scratch_shapes=scratch(n, rows, model, units, pad),
+        scratch_shapes=scratch(n, rows, model, units, pad, hot),
         compiler_params=pltpu.CompilerParams(
             collective_id=0, has_side_effects=True, vmem_limit_bytes=64 * 2**20 - 2**17
         ),
-    )(tokens.reshape(rows, model), table, w_gate[0], w_up[0], w_down[0], joined)
+    )(
+        tokens.reshape(rows, model), jnp.transpose(cold_routes, (2, 0, 1)), hot_pick,
+        jnp.swapaxes(gates, 1, 2),
+        w_gate[0], w_up[0], w_down[0],
+        *(jnp.swapaxes(w, 1, 2) for w in (hot_gate, hot_up, hot_down)),
+    )
     return mixed.reshape(tokens.shape)
 
 

time: 142 us -> 138 us (0.972)
  local copies, waits for them, and re-layouts: 13.2 us -> 1.88 us
  Pallas kernels: 128 us -> 136 us
    pallas_call x1, Pallas kernels: 128 us -> 136 us  [shards(): pl.pallas_call(functools.partial(fused, n, hot, part), out_shape=jax.Shap...]
    concatenate x2 -> x0, local copies, waits for them, and re-layouts: 6.38 us -> none  [the longest x1 6.31 us: shards(): jnp.concatenate([v for w in (hot_gate, hot_up, hot_down) for v in [w[h] f...]
    unnamed x16 -> x1, local copies, waits for them, and re-layouts: 4.29 us -> 1.88 us
    slice x5 -> x0, local copies, waits for them, and re-layouts: 2.19 us -> none  [the longest x3 2.18 us: shards(): w[h]]
where the time goes in v3:
time: 138 us
  Pallas kernels  136 us (99%)
  local copies, waits for them, and re-layouts  1.88 us (1%)
    pallas_call x1, Pallas kernels, shards(): pl.pallas_call(functools.partial(fused, n, hot, part), out_shape=jax.Shap...  136 us

profile of v3, /device:TPU:0, one launch (start us, length us, event | category | flops | bytes accessed | tf_op | source)
XLA Modules:
  0.0 138.3 jit_solution(17898050841487992460)
XLA Ops:
  0.0 136.4 %shard_map.100 = bf16[128,2048]{1,0:T(8,128)(2,1)} custom-call(bf16[128,2048]{1,0:T(8,128)(2,1)} %bitcast.14, s32[7,2,64]{2,1,0:T(2,128)} %bitcast.19, s32[2,64]{1,0:T(2,128)} %pick.1, f32[2,8,64]{2,1,0:T(8,128)} %bitcast.18, bf16[2048,768]{1,0:T(8,128)(2,1)} %bitcast.10, bf16[2048,768]{1,0:T(8,128)(2,1)} %bitcast.11, bf16[768,2048]{1,0:T(8,128)(2,1)} %bitcast.12, ...), custom_call_target="tpu_custom_call" | custom-call | tf_op jit(solution)/shard_map/pallas_call | solution.py:592
  136.4 1.9 %copy.12 = bf16[2,64,2048]{2,1,0:T(8,128)(2,1)} copy(bf16[2,64,2048]{2,1,0:T(8,128)(2,1)} %bitcast.13) | data formatting | bytes 1048576

commit v4 on v2

--- a/solution.py
+++ b/solution.py
@@ -113,8 +113,8 @@
 
 
 def fused(
-    n, hot, part, tok, ct, wg_in, wu_in, wd_in, wh_in, out,
-    xs, keep, sc, rc, sy, ry, sz, rz, wg, wu, wd, wh, hid, hhid, cs,
+    n, hot, part, tok, routes, pick, gts, wg_in, wu_in, wd_in, hg_in, hu_in, hd_in, out,
+    xs, keep, sc, rc, sy, ry, sz, rz, wg, wu, wd, wh, hid, hhid, cs, ct,
     wsem, tsem, cts, ctr, up_s, down_s, z_r, y_s, y_r, c_s, c_r,
     rc_s, rc_r, ry_s, ry_r, rz_s, rz_r,
 ):
@@ -140,7 +140,13 @@
 
     loads = [
         pltpu.make_async_copy(src, dst, wsem.at[i])
-        for i, (src, dst) in enumerate(((wg_in, wg), (wu_in, wu), (wd_in, wd), (wh_in, wh)))
+        for i, (src, dst) in enumerate((
+            *(
+                (src.at[h], wh.at[pl.ds(t * pad + h * part, part)])
+                for t, src in enumerate((hg_in, hu_in, hd_in)) for h in range(hot)
+            ),
+            (wg_in, wg), (wu_in, wu), (wd_in, wd),
+        ))
     ]
     first = pltpu.make_async_copy(tok, xs.at[z, own], tsem)
     first.start()
@@ -186,12 +192,11 @@
         def _():
             go_down(p).start()
 
-        go_y(p).start()
-        go_c(p, 0).start()
-
     def landed(p):
         remote(xs.at[p, own], xs.at[p, own], up_s.at[p], z_r.at[p], me).wait_recv()
         spread(p)
+        go_y(p).start()
+        go_c(p, 0).start()
 
     def plane(s):
         near = jnp.minimum(z, nz - 1 - z)
@@ -231,7 +236,9 @@
             hid[:, cols] = (g / (1.0 + jnp.exp(-g)) * u).astype(jnp.bfloat16)
 
         v = x[...].reshape(4 * rows, model)
-        gu = jnp.dot(v, wh[:, : 2 * pad], preferred_element_type=jnp.float32)
+        gu = lax.dot_general(
+            v, wh[: 2 * pad, :], (((1,), (1,)), ((), ())), preferred_element_type=jnp.float32
+        )
         g, u = gu[:, :pad], gu[:, pad:]
         lane = lax.broadcasted_iota(jnp.int32, (rows, pad), 1)
         warm = []
@@ -251,10 +258,7 @@
             cols = pl.ds(pl.multiple_of(k * tile, tile), tile)
             r = jnp.dot(hid[...], wd[:, cols], preferred_element_type=jnp.float32)
             r = r.astype(jnp.bfloat16).astype(jnp.float32) * cold_c
-            r = r + lax.dot_general(
-                hhid[...], wh[cols, 2 * pad :], (((1,), (1,)), ((), ())),
-                preferred_element_type=jnp.float32,
-            )
+            r = r + jnp.dot(hhid[...], wh[2 * pad :, cols], preferred_element_type=jnp.float32)
             for j in range(2):
                 low = r[2 * j * rows : (2 * j + 1) * rows]
                 high = r[(2 * j + 1) * rows : (2 * j + 2) * rows]
@@ -302,6 +306,37 @@
 
     first.wait()
     spread(z)
+    go_y(z).start()
+    go_c(z, 0).start()
+
+    if pad > hot * part:
+        for t in range(3):
+            blank = wh.at[pl.ds(t * pad + hot * part, pad - hot * part)]
+            blank[...] = jnp.zeros_like(blank)
+
+    ct[...] = jnp.zeros_like(ct)
+    micros = gts.shape[0]
+
+    def joined(parts):
+        return jnp.concatenate(parts, axis=1)
+
+    warm_row = joined([gts[m, 0:1, :] for m in range(micros)])
+    chosen = joined([pick[m : m + 1, :] for m in range(micros)])
+    named = [
+        (
+            joined([routes[k, m : m + 1, :] for m in range(micros)]),
+            joined([gts[m, k + 1 : k + 2, :] for m in range(micros)]),
+        )
+        for k in range(routes.shape[0])
+    ]
+
+    def row(e):
+        return sum(jnp.where(route == e, weight, 0.0) for route, weight in named)
+
+    for e in range(n):
+        ct[e, 0:1, :] = row(e)
+        for h in range(hot):
+            ct[e, 1 + h : 2 + h, :] = jnp.where(chosen == h, warm_row, 0.0)
 
     @pl.loop(1, n)
     def _(i):
@@ -409,7 +444,7 @@
                 share_z(1, p, q).wait_send()
 
 
-def scratch(n, rows, model, units, pad):
+def scratch(n, rows, model, units, pad, hot):
     nz = n // 4
     half, full = jnp.bfloat16, jnp.float32
     dma = pltpu.SemaphoreType.DMA
@@ -425,11 +460,12 @@
         pltpu.VMEM((model, units), half),
         pltpu.VMEM((model, units), half),
         pltpu.VMEM((units, model), half),
-        pltpu.VMEM((model, 3 * pad), half),
+        pltpu.VMEM((3 * pad, model), half),
         pltpu.VMEM((4 * rows, units), half),
         pltpu.VMEM((4 * rows, pad), half),
         pltpu.VMEM((n, 8, rows), full),
-        dma((4,)), dma, dma((n,)), dma((n,)),
+        pltpu.VMEM((n, 8, rows), full),
+        dma((3 + 3 * hot,)), dma, dma((n,)), dma((n,)),
         dma((nz,)), dma((nz,)), dma((nz,)), dma((nz,)), dma((nz,)), dma((nz, 2)), dma((nz, 2)),
         dma((nz, 2, QUARTERS)), dma((nz, 2, QUARTERS)),
         dma((nz, QUARTERS)), dma((nz, QUARTERS)),
@@ -444,37 +480,27 @@
     hot, units, part = hot_gate.shape[0], w_gate.shape[2], hot_gate.shape[2]
     pad = -(-hot * part // 128) * 128
     need = rows * model * n * 9 // 2 * 2 + 3 * model * (units + pad) * 2
-    if n % 4 or rows % 64 or need > ROOM or hot > 7:
+    if n % 4 or part % 16 or rows % 64 or model % 256 or need > ROOM or hot > 7:
         return routed(
             tokens, w_gate, w_up, w_down, hot_gate, hot_up, hot_down, cold_routes, hot_pick, gates
         )
-    routes = cold_routes.reshape(rows, -1).T
-    weights = gates.reshape(rows, -1).T
-    chosen = routes[None] == jnp.arange(n, dtype=jnp.int32)[:, None, None]
-    cold = jnp.sum(jnp.where(chosen, weights[None, 1:], 0.0), axis=1)
-    warm = hot_pick.reshape(1, rows) == jnp.arange(hot, dtype=jnp.int32)[:, None]
-    warm = jnp.where(warm, weights[:1], 0.0)
-    table = jnp.concatenate(
-        [cold[:, None], jnp.broadcast_to(warm[None], (n, hot, rows)),
-         jnp.zeros((n, 7 - hot, rows), jnp.float32)], axis=1,
-    )
-    blank = [jnp.zeros((model, pad - hot * part), jnp.bfloat16)] if pad > hot * part else []
-    joined = jnp.concatenate(
-        [v for w in (hot_gate, hot_up, hot_down) for v in [w[h] for h in range(hot)] + blank],
-        axis=1,
-    )
     anyplace = pl.BlockSpec(memory_space=pl.ANY)
     vmem = pl.BlockSpec(memory_space=pltpu.VMEM)
     mixed = pl.pallas_call(
         functools.partial(fused, n, hot, part),
         out_shape=jax.ShapeDtypeStruct((rows, model), jnp.bfloat16),
-        in_specs=[anyplace, vmem, anyplace, anyplace, anyplace, anyplace],
+        in_specs=[anyplace, vmem, vmem, vmem] + [anyplace] * 6,
         out_specs=vmem,
-        scratch_shapes=scratch(n, rows, model, units, pad),
+        scratch_shapes=scratch(n, rows, model, units, pad, hot),
         compiler_params=pltpu.CompilerParams(
             collective_id=0, has_side_effects=True, vmem_limit_bytes=64 * 2**20 - 2**17
         ),
-    )(tokens.reshape(rows, model), table, w_gate[0], w_up[0], w_down[0], joined)
+    )(
+        tokens.reshape(rows, model), jnp.transpose(cold_routes, (2, 0, 1)), hot_pick,
+        jnp.swapaxes(gates, 1, 2),
+        w_gate[0], w_up[0], w_down[0],
+        *(jnp.swapaxes(w, 1, 2) for w in (hot_gate, hot_up, hot_down)),
+    )
     return mixed.reshape(tokens.shape)
 
 

time: 142 us -> 130 us (0.915)
  local copies, waits for them, and re-layouts: 13.2 us -> 1.88 us
    concatenate x2 -> x0, local copies, waits for them, and re-layouts: 6.38 us -> none  [the longest x1 6.31 us: shards(): jnp.concatenate([v for w in (hot_gate, hot_up, hot_down) for v in [w[h] f...]
    unnamed x16 -> x1, local copies, waits for them, and re-layouts: 4.29 us -> 1.88 us
    slice x5 -> x0, local copies, waits for them, and re-layouts: 2.19 us -> none  [the longest x3 2.18 us: shards(): w[h]]
where the time goes in v4:
time: 130 us
  Pallas kernels  128 us (98%)
  local copies, waits for them, and re-layouts  1.88 us (1%)
    pallas_call x1, Pallas kernels, shards(): pl.pallas_call(functools.partial(fused, n, hot, part), out_shape=jax.Shap...  128 us

profile of v4, /device:TPU:0, one launch (start us, length us, event | category | flops | bytes accessed | tf_op | source)
XLA Modules:
  0.0 129.9 jit_solution(17919266573299877713)
XLA Ops:
  0.0 128.0 %shard_map.100 = bf16[128,2048]{1,0:T(8,128)(2,1)} custom-call(bf16[128,2048]{1,0:T(8,128)(2,1)} %bitcast.14, s32[7,2,64]{2,1,0:T(2,128)} %bitcast.19, s32[2,64]{1,0:T(2,128)} %pick.1, f32[2,8,64]{2,1,0:T(8,128)} %bitcast.18, bf16[2048,768]{1,0:T(8,128)(2,1)} %bitcast.10, bf16[2048,768]{1,0:T(8,128)(2,1)} %bitcast.11, bf16[768,2048]{1,0:T(8,128)(2,1)} %bitcast.12, ...), custom_call_target="tpu_custom_call" | custom-call | tf_op jit(solution)/shard_map/pallas_call | solution.py:489
  128.0 1.9 %copy.12 = bf16[2,64,2048]{2,1,0:T(8,128)(2,1)} copy(bf16[2,64,2048]{2,1,0:T(8,128)(2,1)} %bitcast.13) | data formatting | bytes 1048576
